TPU v7x, 32 devices: a whole 2x2x4 slice. The times are simulated.
32 devices in a mesh: groups: 2 (over y), chan: 4 (over z), tm: 2 (over x), sub: 2 (over core).
Axes of the slice: x: 2, y: 2, z: 4, core: 2. Of those that a mesh axis runs over, the one named last changes fastest.
Arguments:
- voltages: bfloat16 [2, 16, 1024, 8192], P(None, ('groups', 'tm'), None, ('chan', 'sub')), parts along dimension 1, may hold values from -200 to 200
- rfi_mask: int32 [16384], P(('groups', 'chan', 'sub')), parts along dimension 0, may hold values 0 or 1
- inner_delay: int32 [8192, 8], replicated, may hold values from 0 to 2
- pick: int32 [64, 128], replicated, may hold values from 0 to 7
- outer_delay: int32 [64, 128], replicated, may hold values from 0 to 2
Outputs:
- dedispersed: float32 [16, 1024, 128], P(('groups', 'tm'), ('chan', 'sub')), parts along dimension 0
There are 2 independent parts, one for each index of `groups`. A program takes and returns all parts, laid end to end along the dimension named above; an argument that names none is the same for every part. Nothing has to cross between parts.
All inputs are finite; a program needn't handle non-finite values. No bound on the sum of `rfi_mask` on one device may be relied on, other than what follows from the above.
Results may differ from a plain program's by a relative error of at most 0.0013.
Values may be sent and summed in bfloat16 or wider, within the bound.
A program may use at most 128 MiB of HBM per device.

v0:
```python
import math

import jax
import jax.numpy as jnp
from jax import lax
from jax.sharding import PartitionSpec as P

NS = 256
EW = 4
BEAMS = 1024
SUBW = 128
DIN = 2
DOUT = 2


eps_norm = 1e-05


def passed_along(shard, axis, by):
    peers = lax.axis_size(axis)
    pairs = [(i, i + by) for i in range(peers) if 0 <= i + by < peers]
    return lax.ppermute(shard, axis, pairs)


def dft_tables(points):
    positions = jnp.arange(points, dtype=jnp.int32)
    products = positions[:, None] * positions[None, :] % points
    angle = products.astype(jnp.float32) * (2.0 * math.pi / points)
    return (jnp.cos(angle).astype(jnp.bfloat16), jnp.sin(angle).astype(jnp.bfloat16))


def east_west(real_part, imag_part):
    re0, re1, re2, re3 = (real_part[:, 0], real_part[:, 1], real_part[:, 2], real_part[:, 3])
    im0, im1, im2, im3 = (imag_part[:, 0], imag_part[:, 1], imag_part[:, 2], imag_part[:, 3])
    beam_real = jnp.stack(
        [
            re0 + re1 + re2 + re3,
            re0 + im1 - re2 - im3,
            re0 - re1 + re2 - re3,
            re0 - im1 - re2 + im3,
        ],
        1,
    )
    beam_imag = jnp.stack(
        [
            im0 + im1 + im2 + im3,
            im0 - re1 - im2 + re3,
            im0 - im1 + im2 - im3,
            im0 + re1 - im2 - re3,
        ],
        1,
    )
    return (beam_real, beam_imag)


def subband_sums(extended, delays, out_rows):
    lead_rows, beam_count, chan_count = extended.shape
    sub_count = chan_count // SUBW
    trials = delays.shape[1]
    grouped = extended.reshape(lead_rows, beam_count, sub_count, SUBW)
    totals = jnp.zeros((out_rows, beam_count, sub_count, trials), jnp.float32)
    for delay_value in range(DIN + 1):
        selector = (delays == delay_value).astype(jnp.bfloat16).reshape(sub_count, SUBW, trials)
        window = grouped[DIN - delay_value : DIN - delay_value + out_rows]
        totals = totals + jnp.einsum(
            "tbsw,swj->tbsj", window, selector, preferred_element_type=jnp.float32
        )
    scaled = totals * (1.0 / math.sqrt(SUBW))
    return scaled.reshape(out_rows, beam_count, sub_count * trials).astype(jnp.bfloat16)


def merge_subbands(partial_value, pick, outer_delay, out_rows):
    lead_rows, beam_count, width_cols = partial_value.shape
    sub_count, trial_count = pick.shape
    trials = width_cols // sub_count
    slot_ids = jnp.arange(trials, dtype=jnp.int32)
    totals = jnp.zeros((out_rows, beam_count, trial_count), jnp.float32)
    for delay_value in range(DOUT + 1):
        chosen = (pick[:, None, :] == slot_ids[None, :, None]) & (
            outer_delay[:, None, :] == delay_value
        )
        selector = chosen.astype(jnp.bfloat16).reshape(width_cols, trial_count)
        window = partial_value[DOUT - delay_value : DOUT - delay_value + out_rows]
        totals = totals + jnp.einsum(
            "tbw,wk->tbk", window, selector, preferred_element_type=jnp.float32
        )
    return totals * (1.0 / math.sqrt(sub_count))


def corner_turn(block):
    result = lax.all_to_all(block, ("chan", "sub"), split_axis=1, concat_axis=2, tiled=True)
    return result


def body(voltages, rfi_mask, inner_delay, pick, outer_delay):
    time_rows = voltages.shape[1]
    local_chans = voltages.shape[3]
    dft_cos, dft_sin = dft_tables(NS)
    kernel = jnp.stack([jnp.stack([dft_cos, -dft_sin], 1), jnp.stack([dft_sin, dft_cos], 1)], 0)
    volt_cube = voltages.reshape(2, time_rows, EW, NS, local_chans)
    fields = jnp.einsum("ptenc,pnom->otemc", volt_cube, kernel, preferred_element_type=jnp.float32)
    beam_real, beam_imag = east_west(fields[0], fields[1])
    intensity = (
        (beam_real * beam_real + beam_imag * beam_imag)
        .astype(jnp.bfloat16)
        .reshape(time_rows, BEAMS, local_chans)
    )
    sample_count = time_rows * lax.axis_size("tm") * BEAMS
    widened = intensity.astype(jnp.float32)
    chan_mean = lax.psum(jnp.sum(widened, axis=(0, 1)), "tm") / sample_count
    centred = widened - chan_mean
    chan_var = lax.psum(jnp.sum(centred * centred, axis=(0, 1)), "tm") / sample_count
    scale_row = lax.rsqrt(chan_var + eps_norm) * rfi_mask.astype(jnp.float32)
    normed = (centred * scale_row).astype(jnp.bfloat16)
    extra_rows = 0
    tail_rows = passed_along(normed[time_rows - DIN - extra_rows :], "tm", 1)
    extended = jnp.concatenate([tail_rows, normed], 0)
    first_chan = lax.axis_index(("chan", "sub")) * local_chans
    local_delays = lax.dynamic_slice_in_dim(inner_delay, first_chan, local_chans, 0)
    partial_value = corner_turn(subband_sums(extended, local_delays, time_rows + extra_rows))
    earlier = passed_along(partial_value[time_rows - DOUT :], "tm", 1)
    partial_value = jnp.concatenate([earlier, partial_value], 0)
    return merge_subbands(partial_value, pick, outer_delay, time_rows)


def solution(mesh):
    placed = (
        P(None, ("groups", "tm"), None, ("chan", "sub")),
        P(("groups", "chan", "sub")),
        P(),
        P(),
        P(),
    )
    return jax.shard_map(
        body,
        mesh=mesh,
        in_specs=placed,
        out_specs=P(("groups", "tm"), ("chan", "sub"), None),
        check_vma=False,
    )
```

profile of v0, /device:TPU:11, one launch (start us, length us, event | category | flops | bytes accessed | tf_op | source)
XLA Modules:
  0.0 277.3 jit_solution(3408049417663491120)
XLA Ops:
  0.0 1.1 sine_convert_fusion
  1.1 1.0 fusion.57
  2.1 20.1 %convolution_bitcast_fusion = f32[2,4,4,256,1024]{4,3,2,1,0:T(8,128)} fusion(bf16[2,4,4,256,1024]{4,3,2,1,0:T(8,128)(2,1)} %bitcast.110, bf16[1,256,2,256]{1,3,0,2:T(8,128)(2,1)S(1)} %get-tuple-element.20, bf16[1,256,2,256]{1,3,0,2:T(8,128)(2,1)S(1)} %get-tuple-element.19), kind=kOutput, calls=%fused_computation | convolution fusion | flops 8590983168 | bytes 50855936 | tf_op jit(solution)/shard_map/ptenc,pnom->otemc/dot_general | solution.py:101
  22.2 17.0 %slice_bitcast_fusion.1 = (f32[4,4,256,1024]{3,2,1,0:T(8,128)S(1)}, f32[4,4,256,1024]{3,2,1,0:T(8,128)}) fusion(f32[2,4,4,256,1024]{4,3,2,1,0:T(8,128)} %convolution_bitcast_fusion), kind=kLoop, calls=%fused_computation.2 | loop fusion | bytes 67108864 | tf_op jit(solution)/shard_map/squeeze | solution.py:102
  39.2 0.0 copy-start
  39.2 4.7 %add_add_fusion.1 = (f32[4,1,256,1024]{3,2,1,0:T(8,128)}, f32[4,1,256,1024]{3,2,1,0:T(8,128)}) fusion(f32[4,4,256,1024]{3,2,1,0:T(8,128)S(1)} %get-tuple-element.11), kind=kLoop, calls=%fused_computation.31 | loop fusion | flops 6291456 | bytes 25165824 | tf_op jit(solution)/shard_map/add | solution.py:37
  43.9 3.6 %copy-done = f32[4,4,256,1024]{3,2,1,0:T(8,128)} copy-done((f32[4,4,256,1024]{3,2,1,0:T(8,128)}, f32[4,4,256,1024]{3,2,1,0:T(8,128)S(1)}, u32[]{:S(2)}) %copy-start) | copy-done | bytes 16777240
  47.5 18.4 %subtract_subtract_fusion.1 = (f32[4,1,256,1024]{3,2,1,0:T(8,128)S(1)}, f32[4,1,256,1024]{3,2,1,0:T(8,128)}, f32[4,1,256,1024]{3,2,1,0:T(8,128)}, f32[4,1,256,1024]{3,2,1,0:T(8,128)}) fusion(f32[4,4,256,1024]{3,2,1,0:T(8,128)} %get-tuple-element.12, f32[4,4,256,1024]{3,2,1,0:T(8,128)} %copy-done), kind=kLoop, calls=%fused_computation.30 | loop fusion | flops 12582912 | bytes 50331648 | tf_op jit(solution)/shard_map/sub | solution.py:38
  65.8 0.0 copy-start.3
  65.8 0.0 copy-start.4
  65.8 0.0 copy-start.5
  65.8 0.0 copy-start.6
  65.8 0.0 copy-start.7
  65.9 9.0 %add_add_fusion = (f32[4,1,256,1024]{3,2,1,0:T(8,128)S(1)}, f32[4,1,256,1024]{3,2,1,0:T(8,128)}) fusion(f32[4,4,256,1024]{3,2,1,0:T(8,128)} %get-tuple-element.12), kind=kLoop, calls=%fused_computation.27 | loop fusion | flops 6291456 | bytes 25165824 | tf_op jit(solution)/shard_map/add | solution.py:46
  74.8 0.0 copy-done.3
  74.8 0.8 copy-done.4
  75.6 1.2 copy-done.5
  76.8 1.2 copy-done.6
  78.0 1.2 copy-done.7
  79.2 8.9 %convert_reduce_fusion = (f32[1024]{0:T(1024)S(1)}, bf16[4,4,256,1024]{3,2,1,0:T(8,128)(2,1)}) fusion(f32[4,1,256,1024]{3,2,1,0:T(8,128)S(1)} %copy-done.3, f32[4,1,256,1024]{3,2,1,0:T(8,128)} %get-tuple-element.16, f32[4,1,256,1024]{3,2,1,0:T(8,128)S(1)} %copy-done.4, f32[4,1,256,1024]{3,2,1,0:T(8,128)S(1)} %get-tuple-element.15, ...), kind=kLoop, calls=%fused_computation.22 | loop fusion | flops 50330624 | bytes 41947136 | tf_op jit(solution)/shard_map/reduce_sum | solution.py:110
  88.1 3.9 %psum.14 = f32[1024]{0:T(1024)S(1)} all-reduce(f32[1024]{0:T(1024)S(1)} %get-tuple-element.5), channel_id=1, replica_groups=mesh['groups'=2,'chan'=4,'tm'=2,'sub'=2] {'tm'}, use_global_device_ids=true, to_apply=%region_1.2 | all-reduce | flops 1024 | bytes 8192 | tf_op jit(solution)/shard_map/psum | solution.py:110
  92.1 11.3 %convert_element_type.116 = f32[4,4,256,1024]{3,2,1,0:T(8,128)} convert(bf16[4,4,256,1024]{3,2,1,0:T(8,128)(2,1)} %get-tuple-element.6) | non-fusion elementwise | flops 4194304 | bytes 25165824 | tf_op jit(solution)/shard_map/convert_element_type | solution.py:109
  103.4 5.6 %multiply_reduce_fusion = f32[1024]{0:T(1024)S(1)} fusion(bf16[4,4,256,1024]{3,2,1,0:T(8,128)(2,1)} %get-tuple-element.6, f32[1024]{0:T(1024)S(1)} %get-tuple-element.25), kind=kLoop, calls=%fused_computation.13 | loop fusion | flops 16776192 | bytes 8396800 | tf_op jit(solution)/shard_map/reduce_sum | solution.py:112
  109.0 3.8 %psum.15 = f32[1024]{0:T(1024)S(1)} all-reduce(f32[1024]{0:T(1024)S(1)} %multiply_reduce_fusion), channel_id=1, replica_groups=mesh['groups'=2,'chan'=4,'tm'=2,'sub'=2] {'tm'}, use_global_device_ids=true, to_apply=%region_3.4 | all-reduce | flops 1024 | bytes 8192 | tf_op jit(solution)/shard_map/psum | solution.py:112
  112.8 0.0 copy-start.10
  112.8 16.4 %copy.24 = f32[4,1024,1024]{1,2,0:T(8,128)} copy(f32[4,1024,1024]{2,1,0:T(8,128)} %bitcast.103) | data formatting | bytes 33554432 | tf_op jit(solution)/shard_map/convert_element_type | solution.py:109
  129.2 0.0 copy-done.10
  129.2 0.0 slice-start
  129.2 0.0 slice-start.1
  129.2 0.0 slice-start.2
  129.2 8.4 %multiply_convert_fusion = bf16[4,1024,1024]{1,2,0:T(8,128)(2,1)S(1)} fusion(f32[4,1024,1024]{1,2,0:T(8,128)} %copy.24, f32[1024]{0:T(1024)S(1)} %convert_multiply_fusion, f32[1024]{0:T(1024)S(1)} %get-tuple-element.25), kind=kLoop, calls=%fused_computation.12 | loop fusion | flops 12582912 | bytes 25174016 | tf_op jit(solution)/shard_map/convert_element_type | solution.py:114
  137.6 0.0 copy-start.1
  137.6 3.2 %copy-done.1 = bf16[4,1024,1024]{1,2,0:T(8,128)(2,1)} copy-done((bf16[4,1024,1024]{1,2,0:T(8,128)(2,1)}, bf16[4,1024,1024]{1,2,0:T(8,128)(2,1)S(1)}, u32[]{:S(2)}) %copy-start.1) | copy-done | bytes 8388632
  140.9 0.0 slice-start.3
  140.9 2.6 slice.88
  143.4 1.4 collective-permute-start
  144.9 0.0 slice-done
  144.9 0.0 slice-done.1
  144.9 0.0 slice-done.2
  144.9 0.0 slice-done.3
  144.9 8.0 %copy.47 = f32[512,8,8,128]{3,2,1,0:T(8,128)} copy(f32[512,8,8,128]{3,1,2,0:T(8,128)S(1)} %bitcast.106) | data formatting | bytes 33554432
  153.0 10.3 %fusion.11 = f32[8,8,4,1024]{3,1,2,0:T(8,128)S(1)} fusion(f32[4,1024,8,128]{3,2,1,0:T(8,128)} %bitcast.107, f32[8,128]{1,0:T(8,128)S(1)} %bitcast.119, f32[8,128]{1,0:T(8,128)S(1)} %get-tuple-element.24, s32[8192,8]{0,1:T(8,128)} %param.7, s32[]{:T(128)S(6)} %select_n.31), kind=kOutput, calls=%fused_computation.23 | convolution fusion | flops 79699968 | bytes 17866756 | tf_op jit(solution)/shard_map/tbsw,swj->tbsj/dot_general | solution.py:65
  163.2 71.7 %collective-permute-done = bf16[2,1024,1024]{1,2,0:T(8,128)(2,1)} collective-permute-done((bf16[2,1024,1024]{1,2,0:T(8,128)(2,1)}, bf16[2,1024,1024]{1,2,0:T(8,128)(2,1)}, u32[]{:S(2)}, u32[]{:S(2)}) %collective-permute-start) | collective-permute-done | bytes 4194336 | tf_op jit(solution)/shard_map/ppermute | solution.py:22
  234.9 0.0 copy-done.2
  234.9 4.2 %fusion.6 = (bf16[4,1024,1024]{1,2,0:T(8,128)(2,1)S(1)}, bf16[4,1024,1024]{1,2,0:T(8,128)(2,1)S(1)}) fusion(bf16[2,1024,1024]{1,2,0:T(8,128)(2,1)} %collective-permute-done, bf16[4,1024,1024]{1,2,0:T(8,128)(2,1)S(1)} %copy-done.2), kind=kLoop, calls=%fused_computation.16 | loop fusion | flops 8388608 | bytes 29360128 | tf_op jit(solution)/shard_map/concatenate | solution.py:117
  239.1 2.0 fusion.7
  241.1 0.0 copy-start.9
  241.1 2.1 fusion.25
  243.2 0.7 copy.28
  243.9 0.7 reshape.188
  244.6 20.9 %all_to_all.18 = bf16[8,2,16384]{2,1,0:T(2,128)(2,1)S(1)} all-to-all(bf16[8,2,16384]{2,1,0:T(2,128)(2,1)S(1)} %reshape.188), channel_id=1, replica_groups=mesh['groups'=2,'chan'=4,'tm'=2,'sub'=2] {'chan','sub'}, dimensions={0} | all-to-all | bytes 1048576 | tf_op jit(solution)/shard_map/all_to_all | solution.py:91
  265.5 0.7 reshape.189
  266.2 0.6 copy.45
  266.9 0.1 copy.33
  267.1 1.3 collective-permute-start.1
  268.4 0.0 copy-done.9
  268.4 0.1 eq.101
  268.5 0.7 copy.46
  269.2 0.2 copy.34
  269.4 0.0 copy-done.8
  269.5 0.3 fusion.41
  269.8 6.0 %collective-permute-done.1 = bf16[2,128,512]{2,1,0:T(8,128)(2,1)S(1)} collective-permute-done((bf16[2,128,512]{2,1,0:T(8,128)(2,1)S(1)}, bf16[2,128,512]{2,1,0:T(8,128)(2,1)S(1)}, u32[]{:S(2)}, u32[]{:S(2)}) %collective-permute-start.1) | collective-permute-done | bytes 262176 | tf_op jit(solution)/shard_map/ppermute | solution.py:22
  275.7 0.4 convolution_add_fusion.1
  276.2 1.1 fusion.28
  (11 shorter events, 0.2 us)
Async XLA Ops:
  39.2 8.3 %copy-start = (f32[4,4,256,1024]{3,2,1,0:T(8,128)}, f32[4,4,256,1024]{3,2,1,0:T(8,128)S(1)}, u32[]{:S(2)}) copy-start(f32[4,4,256,1024]{3,2,1,0:T(8,128)S(1)} %get-tuple-element.11) | copy-start | bytes 50331652
  65.8 9.0 %copy-start.3 = (f32[4,1,256,1024]{3,2,1,0:T(8,128)S(1)}, f32[4,1,256,1024]{3,2,1,0:T(8,128)}, u32[]{:S(2)}) copy-start(f32[4,1,256,1024]{3,2,1,0:T(8,128)} %get-tuple-element.8) | copy-start | bytes 12582916
  65.8 9.8 %copy-start.4 = (f32[4,1,256,1024]{3,2,1,0:T(8,128)S(1)}, f32[4,1,256,1024]{3,2,1,0:T(8,128)}, u32[]{:S(2)}) copy-start(f32[4,1,256,1024]{3,2,1,0:T(8,128)} %get-tuple-element.9) | copy-start | bytes 12582916
  65.8 11.0 %copy-start.5 = (f32[4,1,256,1024]{3,2,1,0:T(8,128)S(1)}, f32[4,1,256,1024]{3,2,1,0:T(8,128)}, u32[]{:S(2)}) copy-start(f32[4,1,256,1024]{3,2,1,0:T(8,128)} %get-tuple-element.10) | copy-start | bytes 12582916
  65.8 12.2 %copy-start.6 = (f32[4,1,256,1024]{3,2,1,0:T(8,128)S(1)}, f32[4,1,256,1024]{3,2,1,0:T(8,128)}, u32[]{:S(2)}) copy-start(f32[4,1,256,1024]{3,2,1,0:T(8,128)} %get-tuple-element.13) | copy-start | bytes 12582916
  65.8 13.4 %copy-start.7 = (f32[4,1,256,1024]{3,2,1,0:T(8,128)S(1)}, f32[4,1,256,1024]{3,2,1,0:T(8,128)}, u32[]{:S(2)}) copy-start(f32[4,1,256,1024]{3,2,1,0:T(8,128)} %get-tuple-element.14) | copy-start | bytes 12582916
  112.8 16.4 %copy-start.10 = (s32[1024]{0:T(1024)S(1)}, s32[1024]{0:T(1024)}, u32[]{:S(2)}) copy-start(s32[1024]{0:T(1024)} %param.6) | copy-start | bytes 12292
  129.2 15.7 %slice-start = ((s8[16777216]{0:T(1024)(128)(4,1)}), s8[4194304]{0:T(1024)(128)(4,1)S(1)}, s32[]{:S(2)}) async-start(s8[16777216]{0:T(1024)(128)(4,1)} %bitcast.104), calls=%async_computation.1 | async-start | bytes 8388608
  129.2 15.7 %slice-start.1 = ((s8[16777216]{0:T(1024)(128)(4,1)}), s8[4194304]{0:T(1024)(128)(4,1)S(1)}, s32[]{:S(2)}) async-start(s8[16777216]{0:T(1024)(128)(4,1)} %bitcast.104), calls=%async_computation.2 | async-start | bytes 8388608
  129.2 15.7 %slice-start.2 = ((s8[16777216]{0:T(1024)(128)(4,1)}), s8[4194304]{0:T(1024)(128)(4,1)S(1)}, s32[]{:S(2)}) async-start(s8[16777216]{0:T(1024)(128)(4,1)} %bitcast.104), calls=%async_computation.3 | async-start | bytes 8388608
  137.6 3.2 %copy-start.1 = (bf16[4,1024,1024]{1,2,0:T(8,128)(2,1)}, bf16[4,1024,1024]{1,2,0:T(8,128)(2,1)S(1)}, u32[]{:S(2)}) copy-start(bf16[4,1024,1024]{1,2,0:T(8,128)(2,1)S(1)} %multiply_convert_fusion) | copy-start | bytes 25165828
  140.9 4.0 %slice-start.3 = ((s8[16777216]{0:T(1024)(128)(4,1)}), s8[4194304]{0:T(1024)(128)(4,1)S(1)}, s32[]{:S(2)}) async-start(s8[16777216]{0:T(1024)(128)(4,1)} %bitcast.104), calls=%async_computation.4 | async-start | bytes 8388608
  143.4 91.5 %collective-permute-start = (bf16[2,1024,1024]{1,2,0:T(8,128)(2,1)}, bf16[2,1024,1024]{1,2,0:T(8,128)(2,1)}, u32[]{:S(2)}, u32[]{:S(2)}) collective-permute-start(bf16[2,1024,1024]{1,2,0:T(8,128)(2,1)} %slice.88), channel_id=1, source_target_pairs={{0,2},{1,3},{4,6},{5,7},{8,10},{9,11},{12,14},{13,15},{16,18},{17,... | collective-permute-start | bytes 12582920 | tf_op jit(solution)/shard_map/ppermute | solution.py:22
  153.0 82.0 %copy-start.2 = (bf16[4,1024,1024]{1,2,0:T(8,128)(2,1)S(1)}, bf16[4,1024,1024]{1,2,0:T(8,128)(2,1)}, u32[]{:S(2)}) copy-start(bf16[4,1024,1024]{1,2,0:T(8,128)(2,1)} %copy-done.1) | copy-start | bytes 25165828
  241.1 27.3 %copy-start.9 = (s32[64,128]{1,0:T(8,128)S(1)}, s32[64,128]{1,0:T(8,128)}, u32[]{:S(2)}) copy-start(s32[64,128]{1,0:T(8,128)} %param.9) | copy-start | bytes 98308
  243.2 26.3 %copy-start.8 = (s32[64,128]{1,0:T(8,128)S(1)}, s32[64,128]{1,0:T(8,128)}, u32[]{:S(2)}) copy-start(s32[64,128]{1,0:T(8,128)} %param.8) | copy-start | bytes 98308
  267.1 8.7 %collective-permute-start.1 = (bf16[2,128,512]{2,1,0:T(8,128)(2,1)S(1)}, bf16[2,128,512]{2,1,0:T(8,128)(2,1)S(1)}, u32[]{:S(2)}, u32[]{:S(2)}) collective-permute-start(bf16[2,128,512]{2,1,0:T(8,128)(2,1)S(1)} %copy.33), channel_id=1, source_target_pairs={{0,2},{1,3},{4,6},{5,7},{8,10},{9,11},{12,14},{13,15},{16,18},{17,... | collective-permute-start | bytes 786440 | tf_op jit(solution)/shard_map/ppermute | solution.py:22
where the time goes:
time: 282 us; the launch traced here: 277 us
  waiting for transfers between devices  77.7 us (28%)
  other arithmetic  72.6 us (26%)
  local copies, waits for them, and re-layouts  59.2 us (21%)
  matrix products  36.2 us (13%)
  blocking collectives  28.6 us (10%)
    ppermute x2, waiting for transfers between devices, passed_along(): return lax.ppermute(shard, axis, pairs)  77.7 us
    all_to_all x1, blocking collectives, corner_turn(): lax.all_to_all(block, ('chan', 'sub'), split_axis=1, concat_axis=2, tiled...  20.9 us
    unnamed x33, local copies, waits for them, and re-layouts  20.6 us
    dot_general x1, matrix products, body(): jnp.einsum('ptenc,pnom->otemc', volt_cube, kernel, preferred_element_type...  20.1 us
    sub x1, other arithmetic, east_west(): re0 + im1 - re2 - im3  18.4 us
    squeeze x1, local copies, waits for them, and re-layouts, body(): beam_real, beam_imag = east_west(fields[0], fields[1])  17 us
    convert_element_type x1, local copies, waits for them, and re-layouts, body(): widened = intensity.astype(jnp.float32)  16.4 us
    dot_general x3, matrix products, subband_sums(): jnp.einsum('tbsw,swj->tbsj', window, selector, preferred_element_type=jnp...  14.3 us
  transfers between devices with their start and end apart: 2, of which 2 were waited for; matrix products, arithmetic and copies ran while one was open for 7% of the time, Pallas kernels for 0%

commit v1 on v0

v1 whole, which is shorter than its diff:
```python
import functools
import math

import jax
import jax.numpy as jnp
import numpy as np
from jax import lax
from jax.experimental import pallas as pl
from jax.experimental.pallas import tpu as pltpu
from jax.sharding import PartitionSpec as P

NS = 256
EW = 4
BEAMS = 1024
SUBW = 128
DIN = 2
DOUT = 2
NJ = 8
LANES = 128

eps_norm = 1e-05
MESH = pl.DeviceIdType.MESH


def dft_matrix(points):
    positions = np.arange(points, dtype=np.int32)
    products = positions[:, None] * positions[None, :] % points
    angle = products.astype(np.float32) * np.float32(2.0 * math.pi / points)
    cos, sin = np.cos(angle), np.sin(angle)
    table = np.concatenate(
        [np.concatenate([cos.T, sin.T], 1), np.concatenate([-sin.T, cos.T], 1)], 0
    )
    return table.astype(jnp.bfloat16)


def kernel(
    cfg,
    volt_hbm,
    table_ref,
    mask_ref,
    delay_hbm,
    pick_ref,
    outer_ref,
    out_ref,
    vbuf,
    inten,
    field0,
    field1,
    delay_v,
    sel1,
    sel2,
    pilot,
    acc1,
    acc2,
    stats,
    part_acc,
    carry_out,
    carry_in,
    send_buf,
    recv_buf,
    carry2_out,
    carry2_in,
    vsem,
    dsem,
    stat_send,
    stat_recv,
    carry_send,
    carry_recv,
    turn_send,
    turn_recv,
    own_sem,
    carry2_send,
    carry2_recv,
):
    rows, chans, ct, ntm, nsub, ndev, ndm = (
        cfg["rows"], cfg["chans"], cfg["ct"], cfg["ntm"], cfg["nsub"], cfg["ndev"], cfg["ndm"],
    )
    pairs = rows // 2
    ctiles = chans // ct
    steps = rows * ctiles
    local_beams = BEAMS // ndev
    subs = chans // SUBW
    width = subs * NJ
    rb_rows = cfg["rb"]
    nrb = BEAMS // rb_rows
    tm = lax.axis_index("tm")
    me = lax.axis_index("chan") * nsub + lax.axis_index("sub")

    def peer_id(index):
        return {"chan": index // nsub, "sub": lax.rem(index, nsub)}

    def volt_copy(step):
        t, tile = step // ctiles, lax.rem(step, ctiles)
        return pltpu.make_async_copy(
            volt_hbm.at[:, t, :, pl.ds(pl.multiple_of(tile * ct, ct), ct)],
            vbuf.at[step],
            vsem.at[step],
        )

    def start_volt(step, carry):
        volt_copy(step).start()
        return carry

    lax.fori_loop(0, steps, start_volt, 0)
    delay_copy = pltpu.make_async_copy(
        delay_hbm.at[:, pl.ds(pl.multiple_of(me * chans, chans), chans)], delay_v, dsem
    )
    delay_copy.start()

    barrier = pltpu.get_barrier_semaphore()

    def greet_tm(k, carry):
        pl.semaphore_signal(
            barrier, inc=1, device_id={"tm": lax.rem(tm + k, ntm)}, device_id_type=MESH
        )
        return carry

    def greet_turn(k, carry):
        pl.semaphore_signal(
            barrier, inc=1, device_id=peer_id(lax.rem(me + k, ndev)), device_id_type=MESH
        )
        return carry

    lax.fori_loop(1, ntm, greet_tm, 0)
    lax.fori_loop(1, ndev, greet_turn, 0)

    delay_copy.wait()
    delays = delay_v[...].astype(jnp.float32)
    chan_sub = lax.broadcasted_iota(jnp.int32, (NJ, chans), 1) // SUBW
    for par_in in range(2):
        for half in range(2):
            pieces = []
            for group in range(LANES // NJ):
                par_out, sub = group // subs, group % subs
                lag = 2 * half + par_out - par_in
                if group < 2 * subs and 0 <= lag <= DIN:
                    hit = (delays == float(lag)) & (chan_sub == sub)
                    pieces.append(jnp.where(hit, 1.0, 0.0))
                else:
                    pieces.append(jnp.zeros((NJ, chans), jnp.float32))
            sel1[par_in, half * LANES : (half + 1) * LANES, :] = jnp.concatenate(
                pieces, 0
            ).astype(jnp.bfloat16)
    nsubs_all = subs * ndev
    code = (pick_ref[...] + NJ * outer_ref[...]).astype(jnp.float32).astype(jnp.bfloat16)

    def make_sel2(dev, carry):
        q = lax.broadcasted_iota(jnp.int32, (LANES, nsubs_all), 0)
        which = dev * subs + lax.rem(q, width) // NJ
        expand = jnp.where(
            which == lax.broadcasted_iota(jnp.int32, (LANES, nsubs_all), 1), 1.0, 0.0
        ).astype(jnp.bfloat16)
        spread = jnp.dot(expand, code, preferred_element_type=jnp.float32)
        q = lax.broadcasted_iota(jnp.int32, (LANES, ndm), 0)
        slot = lax.rem(q, NJ)
        par_in = q // width
        base = pl.multiple_of(dev * LANES, LANES)
        for half in range(2):
            for par_out in range(2):
                lag = 2 * half + par_out - par_in
                want = (slot + NJ * lag).astype(jnp.float32)
                hit = (spread == want) & (lag >= 0) & (lag <= DOUT) & (par_in < 2)
                col = (2 * half + par_out) * ndm
                sel2[pl.ds(base, LANES), col : col + ndm] = jnp.where(hit, 1.0, 0.0).astype(
                    jnp.bfloat16
                )
        return carry

    lax.fori_loop(0, ndev, make_sel2, 0)
    pilot[...] = jnp.zeros_like(pilot)
    acc1[...] = jnp.zeros_like(acc1)
    acc2[...] = jnp.zeros_like(acc2)

    @pl.when(tm == 0)
    def _():
        carry_in[...] = jnp.zeros_like(carry_in)
        carry2_in[...] = jnp.zeros_like(carry2_in)

    def transform(step, field):
        volt_copy(step).wait()
        for e in range(EW):
            block = vbuf[step, :, e * NS : (e + 1) * NS, :].reshape(2 * NS, ct)
            field[e] = jnp.dot(table_ref[...], block, preferred_element_type=jnp.float32)

    CH = 16

    def fold8(x):
        return x[:8] + x[8:]

    def detect(step, field):
        t, tile = step // ctiles, lax.rem(step, ctiles)
        shift = jnp.broadcast_to(pilot[tile], (CH, ct))
        s1 = jnp.zeros((8, ct), jnp.float32)
        s2 = jnp.zeros((8, ct), jnp.float32)
        col = pl.ds(pl.multiple_of(tile * ct, ct), ct)
        for chunk in range(NS // CH):
            lo = chunk * CH
            re = [field[e, lo : lo + CH, :] for e in range(EW)]
            im = [field[e, NS + lo : NS + lo + CH, :] for e in range(EW)]
            ra, rb, rc, rd = re[0] + re[2], re[0] - re[2], re[1] + re[3], re[1] - re[3]
            ia, ib, ic, id_ = im[0] + im[2], im[0] - im[2], im[1] + im[3], im[1] - im[3]
            beam = [
                (ra + rc, ia + ic),
                (rb + id_, ib - rd),
                (ra - rc, ia - ic),
                (rb - id_, ib + rd),
            ]
            for q in range(EW):
                x = beam[q][0] * beam[q][0] + beam[q][1] * beam[q][1]
                x = x.astype(jnp.bfloat16)
                inten[t, q * NS + lo : q * NS + lo + CH, col] = x
                dev = x.astype(jnp.float32) - shift
                s1 = s1 + fold8(dev)
                s2 = s2 + fold8(dev * dev)

        @pl.when(t > 0)
        def _():
            acc1[tile] += s1
            acc2[tile] += s2

        @pl.when(t == 0)
        def _():
            mean = jnp.sum(s1, axis=0, keepdims=True) * (1.0 / BEAMS)
            pilot[tile] = mean
            wide = jnp.broadcast_to(mean, (CH, ct))

            def again(chunk, sums):
                r1, r2 = sums
                lo = pl.multiple_of(chunk * 4 * CH, 4 * CH)
                for i in range(4):
                    x = inten[0, pl.ds(lo + i * CH, CH), col].astype(jnp.float32)
                    dev = x - wide
                    r1 = r1 + fold8(dev)
                    r2 = r2 + fold8(dev * dev)
                return r1, r2

            zero = jnp.zeros((8, ct), jnp.float32)
            r1, r2 = lax.fori_loop(0, BEAMS // (4 * CH), again, (zero, zero))
            acc1[tile] = r1
            acc2[tile] = r2

    transform(0, field0)

    def two_steps(i, carry):
        transform(2 * i + 1, field1)
        detect(2 * i, field0)

        @pl.when(2 * i + 2 < steps)
        def _():
            transform(2 * i + 2, field0)

        detect(2 * i + 1, field1)
        return carry

    lax.fori_loop(0, steps // 2, two_steps, 0)

    count = float(rows * BEAMS)
    for tile in range(ctiles):
        s1 = jnp.sum(acc1[tile], axis=0, keepdims=True)
        s2 = jnp.sum(acc2[tile], axis=0, keepdims=True)
        cols = slice(tile * ct, (tile + 1) * ct)
        stats[tm, 0:1, cols] = pilot[tile] + s1 * (1.0 / count)
        stats[tm, 1:2, cols] = s2 - s1 * s1 * (1.0 / count)

    pl.semaphore_wait(barrier, ntm - 1 + ndev - 1)

    def stat_copy(k, sender):
        return pltpu.make_async_remote_copy(
            src_ref=stats.at[tm],
            dst_ref=stats.at[sender],
            send_sem=stat_send.at[k],
            recv_sem=stat_recv.at[k],
            device_id={"tm": lax.rem(tm + k, ntm)},
            device_id_type=MESH,
        )

    for k in range(1, ntm):
        stat_copy(k, tm).start()
    for k in range(1, ntm):
        stat_copy(k, lax.rem(tm + ntm - k, ntm)).wait_recv()
    means = [stats[i, 0:1, :] for i in range(ntm)]
    mean = sum(means[1:], means[0]) * (1.0 / ntm)
    spread = sum(stats[i, 1:2, :] for i in range(ntm))
    for i in range(ntm):
        spread = spread + count * ((means[i] - mean) * (means[i] - mean))
    var = spread * (1.0 / (count * ntm))
    scale = lax.rsqrt(var + eps_norm) * mask_ref[...].astype(jnp.float32)

    def carry_copy(rb):
        return pltpu.make_async_remote_copy(
            src_ref=carry_out.at[rb],
            dst_ref=carry_in.at[rb],
            send_sem=carry_send.at[rb],
            recv_sem=carry_recv.at[rb],
            device_id={"tm": lax.rem(tm + 1, ntm)},
            device_id_type=MESH,
        )

    def level1(pair, rb):
        lo = pl.multiple_of(rb * rb_rows, rb_rows)
        total = None
        for par in range(2):
            x = inten[2 * pair + par, pl.ds(lo, rb_rows), :].astype(jnp.float32)
            normed = ((x - mean) * scale).astype(jnp.bfloat16)
            term = lax.dot_general(
                normed, sel1[par], (((1,), (1,)), ((), ())), preferred_element_type=jnp.float32
            )
            total = term if total is None else total + term
        return lo, total

    inv1 = 1.0 / math.sqrt(SUBW)

    def put_send(pair, lo, total):
        send_buf[pair, pl.ds(lo, rb_rows), :] = (total * inv1).astype(jnp.bfloat16)

    def turn_copy(pair, k, sender):
        peer = lax.rem(me + k, ndev)
        return pltpu.make_async_remote_copy(
            src_ref=send_buf.at[
                pair, pl.ds(pl.multiple_of(peer * local_beams, local_beams), local_beams), :
            ],
            dst_ref=recv_buf.at[pair, :, pl.ds(pl.multiple_of(sender * LANES, LANES), LANES)],
            send_sem=turn_send.at[pair, k],
            recv_sem=turn_recv.at[pair, k],
            device_id=peer_id(peer),
            device_id_type=MESH,
        )

    def own_copy(pair):
        return pltpu.make_async_copy(
            send_buf.at[
                pair, pl.ds(pl.multiple_of(me * local_beams, local_beams), local_beams), :
            ],
            recv_buf.at[pair, :, pl.ds(pl.multiple_of(me * LANES, LANES), LANES)],
            own_sem.at[pair],
        )

    def start_turn(pair):
        def one(k, carry):
            turn_copy(pair, k, me).start()
            return carry

        lax.fori_loop(1, ndev, one, 0)
        own_copy(pair).start()

    last = pairs - 1
    for pair in range(last, -1, -1):

        def block(rb, carry, pair=pair):
            lo, total = level1(pair, rb)
            if pair == last:
                carry_out[rb] = total[:, LANES:]

                @pl.when(tm < ntm - 1)
                def _():
                    carry_copy(rb).start()

            else:
                put_send(pair + 1, lo, part_acc[pair + 1, pl.ds(lo, rb_rows), :] + total[:, LANES:])
            part_acc[pair, pl.ds(lo, rb_rows), :] = total[:, :LANES]
            return carry

        lax.fori_loop(0, nrb, block, 0)
        if pair < last:
            start_turn(pair + 1)

    def finish(rb, carry):
        @pl.when(tm > 0)
        def _():
            carry_copy(rb).wait_recv()

        lo = pl.multiple_of(rb * rb_rows, rb_rows)
        put_send(0, lo, part_acc[0, pl.ds(lo, rb_rows), :] + carry_in[rb])
        return carry

    lax.fori_loop(0, nrb, finish, 0)
    start_turn(0)

    carry2_copy = pltpu.make_async_remote_copy(
        src_ref=carry2_out,
        dst_ref=carry2_in,
        send_sem=carry2_send,
        recv_sem=carry2_recv,
        device_id={"tm": lax.rem(tm + 1, ntm)},
        device_id_type=MESH,
    )
    inv2 = 1.0 / math.sqrt(nsubs_all)
    held = None
    for pair in range(last, -1, -1):

        def arrive(k, carry, pair=pair):
            turn_copy(pair, k, lax.rem(me + ndev - k, ndev)).wait_recv()
            return carry

        lax.fori_loop(1, ndev, arrive, 0)
        own_copy(pair).wait()
        merged = jnp.dot(recv_buf[pair], sel2[...], preferred_element_type=jnp.float32)
        if pair == last:
            carry2_out[...] = merged[:, 2 * ndm :]

            @pl.when(tm < ntm - 1)
            def _():
                carry2_copy.start()

        else:
            held = held + merged[:, 2 * ndm :]
            out_ref[2 * pair + 2] = held[:, :ndm] * inv2
            out_ref[2 * pair + 3] = held[:, ndm:] * inv2
        held = merged[:, : 2 * ndm]

    @pl.when(tm > 0)
    def _():
        carry2_copy.wait_recv()

    held = held + carry2_in[...]
    out_ref[0] = held[:, :ndm] * inv2
    out_ref[1] = held[:, ndm:] * inv2

    for k in range(1, ntm):
        stat_copy(k, tm).wait_send()

    @pl.when(tm < ntm - 1)
    def _():
        def sent(rb, carry):
            carry_copy(rb).wait_send()
            return carry

        lax.fori_loop(0, nrb, sent, 0)
        carry2_copy.wait_send()

    for pair in range(pairs):

        def left(k, carry, pair=pair):
            turn_copy(pair, k, me).wait_send()
            return carry

        lax.fori_loop(1, ndev, left, 0)


def body(voltages, rfi_mask, inner_delay, pick, outer_delay):
    rows, chans = voltages.shape[1], voltages.shape[3]
    ntm, nsub = lax.axis_size("tm"), lax.axis_size("sub")
    ndev = lax.axis_size("chan") * nsub
    ndm = pick.shape[1]
    ct = min(256, chans)
    ctiles = chans // ct
    pairs = rows // 2
    rb = 256
    nrb = BEAMS // rb
    lb = BEAMS // ndev
    cfg = dict(rows=rows, chans=chans, ct=ct, ntm=ntm, nsub=nsub, ndev=ndev, ndm=ndm, rb=rb)
    f32, bf16 = jnp.float32, jnp.bfloat16
    vm = pl.BlockSpec(memory_space=pltpu.VMEM)
    hbm = pl.BlockSpec(memory_space=pl.ANY)
    dma, steps = pltpu.SemaphoreType.DMA, rows * ctiles
    return pl.pallas_call(
        functools.partial(kernel, cfg),
        out_shape=jax.ShapeDtypeStruct((rows, lb, ndm), f32),
        in_specs=[hbm, vm, vm, hbm, vm, vm],
        out_specs=vm,
        scratch_shapes=[
            pltpu.VMEM((steps, 2, EW * NS, ct), bf16),
            pltpu.VMEM((rows, BEAMS, chans), bf16),
            pltpu.VMEM((EW, 2 * NS, ct), f32),
            pltpu.VMEM((EW, 2 * NS, ct), f32),
            pltpu.VMEM((NJ, chans), jnp.int32),
            pltpu.VMEM((2, 2 * LANES, chans), bf16),
            pltpu.VMEM((ndev * LANES, 4 * ndm), bf16),
            pltpu.VMEM((ctiles, 1, ct), f32),
            pltpu.VMEM((ctiles, 8, ct), f32),
            pltpu.VMEM((ctiles, 8, ct), f32),
            pltpu.VMEM((ntm, 2, chans), f32),
            pltpu.VMEM((pairs, BEAMS, LANES), f32),
            pltpu.VMEM((nrb, rb, LANES), f32),
            pltpu.VMEM((nrb, rb, LANES), f32),
            pltpu.VMEM((pairs, BEAMS, LANES), bf16),
            pltpu.VMEM((pairs, lb, ndev * LANES), bf16),
            pltpu.VMEM((lb, 2 * ndm), f32),
            pltpu.VMEM((lb, 2 * ndm), f32),
            dma((steps,)),
            dma,
            dma((ntm,)),
            dma((ntm,)),
            dma((nrb,)),
            dma((nrb,)),
            dma((pairs, ndev)),
            dma((pairs, ndev)),
            dma((pairs,)),
            dma,
            dma,
        ],
        compiler_params=pltpu.CompilerParams(
            collective_id=0, has_side_effects=True, vmem_limit_bytes=60 * 2**20
        ),
    )(
        voltages,
        jnp.asarray(dft_matrix(NS)),
        rfi_mask.reshape(1, chans),
        inner_delay.T,
        pick,
        outer_delay,
    )


def solution(mesh):
    placed = (
        P(None, ("groups", "tm"), None, ("chan", "sub")),
        P(("groups", "chan", "sub")),
        P(),
        P(),
        P(),
    )
    return jax.shard_map(
        body,
        mesh=mesh,
        in_specs=placed,
        out_specs=P(("groups", "tm"), ("chan", "sub"), None),
        check_vma=False,
    )
```

time: 282 us -> 50.6 us (0.18); the launches traced: 277 us -> 50.1 us
  waiting for transfers between devices: 77.7 us -> 0 us
  other arithmetic: 72.6 us -> 0 us
  local copies, waits for them, and re-layouts: 59.2 us -> 1.67 us
  Pallas kernels: 0 us -> 48.4 us
  matrix products: 36.2 us -> 0 us
  blocking collectives: 28.6 us -> 0 us
    ppermute x2 -> x0, waiting for transfers between devices: 77.7 us -> none  [passed_along(): return lax.ppermute(shard, axis, pairs)]
    pallas_call x0 -> x1, Pallas kernels: none -> 48.4 us  [body(): pl.pallas_call(functools.partial(kernel, cfg), out_shape=jax.ShapeDtypeSt...]
    dot_general x7 -> x0, matrix products: 36.2 us -> none  [the longest x1 20.1 us: body(): jnp.einsum('ptenc,pnom->otemc', volt_cube, kernel, preferred_element_type...]
    all_to_all x1 -> x0, blocking collectives: 20.9 us -> none  [corner_turn(): lax.all_to_all(block, ('chan', 'sub'), split_axis=1, concat_axis=2, tiled...]
    convert_element_type x3 -> x0, other arithmetic: 20.8 us -> none  [the longest x1 11.3 us: body(): widened = intensity.astype(jnp.float32)]
    unnamed x33 -> x1, local copies, waits for them, and re-layouts: 20.6 us -> 1.67 us
    sub x2 -> x0, other arithmetic: 18.4 us -> none  [the longest x1 18.4 us: east_west(): re0 + im1 - re2 - im3]
    convert_element_type x3 -> x0, local copies, waits for them, and re-layouts: 17.2 us -> none  [the longest x1 16.4 us: body(): widened = intensity.astype(jnp.float32)]
  transfers between devices with their start and end apart: 2 -> 0, of which waited for: 2 -> 0; matrix products, arithmetic and copies ran while one was open for 7% -> 0% of each run, Pallas kernels for 0% -> 0%
where the time goes in v1:
time: 50.6 us; the launch traced here: 50.1 us
  Pallas kernels  48.4 us (96%)
  local copies, waits for them, and re-layouts  1.67 us (3%)
    pallas_call x1, Pallas kernels, body(): pl.pallas_call(functools.partial(kernel, cfg), out_shape=jax.ShapeDtypeSt...  48.4 us
    unnamed x1, local copies, waits for them, and re-layouts  1.67 us

profile of v1, /device:TPU:11, one launch (start us, length us, event | category | flops | bytes accessed | tf_op | source)
XLA Modules:
  0.0 50.1 jit_solution(15813397011224440937)
XLA Ops:
  0.0 48.4 %shard_map.64 = f32[4,128,128]{2,1,0:T(8,128)} custom-call(bf16[2,4,1024,1024]{3,2,1,0:T(8,128)(2,1)} %volt_hbm.1, bf16[512,512]{1,0:T(8,128)(2,1)} %constant.2.clone.table_ref, s32[1,1024]{1,0:T(1,128)} %bitcast.3, s32[8,8192]{1,0:T(8,128)} %bitcast.2, s32[64,128]{1,0:T(8,128)} %pick_ref.1, s32[64,128]{1,0:T(8,128)} %outer_ref.1), custom_call_target="tpu_custom_call" | custom-call | tf_op jit(solution)/shard_map/pallas_call | solution.py:456
  48.5 1.7 %copy.8 = f32[4,128,128]{2,1,0:T(8,128)} copy(f32[4,128,128]{2,1,0:T(8,128)} %shard_map.64) | data formatting | bytes 524288

commit v2 on v1

--- a/solution.py
+++ b/solution.py
@@ -26,10 +26,9 @@
     positions = np.arange(points, dtype=np.int32)
     products = positions[:, None] * positions[None, :] % points
     angle = products.astype(np.float32) * np.float32(2.0 * math.pi / points)
+    half = points // 2
     cos, sin = np.cos(angle), np.sin(angle)
-    table = np.concatenate(
-        [np.concatenate([cos.T, sin.T], 1), np.concatenate([-sin.T, cos.T], 1)], 0
-    )
+    table = np.concatenate([cos[:half], cos[half : half + 1], sin[1:half]], 0)
     return table.astype(jnp.bfloat16)
 
 
@@ -124,6 +123,146 @@
     lax.fori_loop(1, ntm, greet_tm, 0)
     lax.fori_loop(1, ndev, greet_turn, 0)
 
+    pilot[...] = jnp.zeros_like(pilot)
+    acc1[...] = jnp.zeros_like(acc1)
+    acc2[...] = jnp.zeros_like(acc2)
+
+    @pl.when(tm == 0)
+    def _():
+        carry_in[...] = jnp.zeros_like(carry_in)
+        carry2_in[...] = jnp.zeros_like(carry2_in)
+
+    def transform(step, field):
+        volt_copy(step).wait()
+        for e in range(EW):
+            for part in range(2):
+                block = vbuf[step, part, e * NS : (e + 1) * NS, :]
+                field[e, part * NS : (part + 1) * NS, :] = jnp.dot(
+                    table_ref[...], block, preferred_element_type=jnp.float32
+                )
+
+    CH, HALF = 16, NS // 2
+
+    def fold8(x):
+        return x[:8] + x[8:]
+
+    def detect(step, field):
+        t, tile = step // ctiles, lax.rem(step, ctiles)
+        col = pl.ds(pl.multiple_of(tile * ct, ct), ct)
+        wide_row = pilot[tile]
+        sums1, sums2 = [], []
+        top = lax.broadcasted_iota(jnp.int32, (CH, LANES), 0) == 0
+        for lane in range(0, ct, LANES):
+            shift = jnp.broadcast_to(wide_row[:, lane : lane + LANES], (CH, LANES))
+            s1 = jnp.zeros((8, LANES), jnp.float32)
+            s2 = jnp.zeros((8, LANES), jnp.float32)
+            here = pl.ds(pl.multiple_of(tile * ct + lane, LANES), LANES)
+            for chunk in range(HALF // CH):
+                lo = chunk * CH
+
+                def part(index):
+                    at = index * HALF + lo
+                    return [field[e, at : at + CH, lane : lane + LANES] for e in range(EW)]
+
+                ca, sb, cb, sa = part(0), part(1), part(2), part(3)
+                if chunk == 0:
+                    sa0 = [jnp.where(top, 0.0, v) for v in sa]
+                    sb0 = [jnp.where(top, 0.0, v) for v in sb]
+                else:
+                    sa0, sb0 = sa, sb
+                for mirror in range(2):
+                    if mirror == 0:
+                        re = [u + v for u, v in zip(ca, sa0)]
+                        im = [u - v for u, v in zip(cb, sb0)]
+                    else:
+                        re = [u - v for u, v in zip(ca, sa0)]
+                        im = [u + v for u, v in zip(cb, sb0)]
+                        if chunk == 0:
+                            re = [jnp.where(top, v, u) for u, v in zip(re, sb)]
+                            im = [jnp.where(top, v, u) for u, v in zip(im, sa)]
+                    ra, rb, rc, rd = re[0] + re[2], re[0] - re[2], re[1] + re[3], re[1] - re[3]
+                    ia, ib, ic, id_ = im[0] + im[2], im[0] - im[2], im[1] + im[3], im[1] - im[3]
+                    beam = [
+                        (ra + rc, ia + ic),
+                        (rb + id_, ib - rd),
+                        (ra - rc, ia - ic),
+                        (rb - id_, ib + rd),
+                    ]
+                    for q in range(EW):
+                        x = beam[q][0] * beam[q][0] + beam[q][1] * beam[q][1]
+                        x = x.astype(jnp.bfloat16)
+                        at = q * NS + mirror * HALF + lo
+                        inten[t, at : at + CH, here] = x
+                        dev = x.astype(jnp.float32) - shift
+                        s1 = s1 + fold8(dev)
+                        s2 = s2 + fold8(dev * dev)
+            sums1.append(s1)
+            sums2.append(s2)
+        s1, s2 = jnp.concatenate(sums1, 1), jnp.concatenate(sums2, 1)
+
+        @pl.when(t > 0)
+        def _():
+            acc1[tile] += s1
+            acc2[tile] += s2
+
+        @pl.when(t == 0)
+        def _():
+            mean = jnp.sum(s1, axis=0, keepdims=True) * (1.0 / BEAMS)
+            pilot[tile] = mean
+            wide = jnp.broadcast_to(mean, (CH, ct))
+
+            def again(chunk, sums):
+                r1, r2 = sums
+                lo = pl.multiple_of(chunk * 4 * CH, 4 * CH)
+                for i in range(4):
+                    x = inten[0, pl.ds(lo + i * CH, CH), col].astype(jnp.float32)
+                    dev = x - wide
+                    r1 = r1 + fold8(dev)
+                    r2 = r2 + fold8(dev * dev)
+                return r1, r2
+
+            zero = jnp.zeros((8, ct), jnp.float32)
+            r1, r2 = lax.fori_loop(0, BEAMS // (4 * CH), again, (zero, zero))
+            acc1[tile] = r1
+            acc2[tile] = r2
+
+    transform(0, field0)
+
+    def two_steps(i, carry):
+        transform(2 * i + 1, field1)
+        detect(2 * i, field0)
+
+        transform(2 * i + 2, field0)
+        detect(2 * i + 1, field1)
+        return carry
+
+    lax.fori_loop(0, steps // 2 - 1, two_steps, 0)
+    transform(steps - 1, field1)
+    detect(steps - 2, field0)
+    detect(steps - 1, field1)
+
+    count = float(rows * BEAMS)
+    for tile in range(ctiles):
+        s1 = jnp.sum(acc1[tile], axis=0, keepdims=True)
+        s2 = jnp.sum(acc2[tile], axis=0, keepdims=True)
+        cols = slice(tile * ct, (tile + 1) * ct)
+        stats[tm, 0:1, cols] = pilot[tile] + s1 * (1.0 / count)
+        stats[tm, 1:2, cols] = s2 - s1 * s1 * (1.0 / count)
+
+    pl.semaphore_wait(barrier, ntm - 1 + ndev - 1)
+
+    def stat_copy(k, sender):
+        return pltpu.make_async_remote_copy(
+            src_ref=stats.at[tm],
+            dst_ref=stats.at[sender],
+            send_sem=stat_send.at[k],
+            recv_sem=stat_recv.at[k],
+            device_id={"tm": lax.rem(tm + k, ntm)},
+            device_id_type=MESH,
+        )
+
+    for k in range(1, ntm):
+        stat_copy(k, tm).start()
     delay_copy.wait()
     delays = delay_v[...].astype(jnp.float32)
     chan_sub = lax.broadcasted_iota(jnp.int32, (NJ, chans), 1) // SUBW
@@ -141,6 +280,112 @@
             sel1[par_in, half * LANES : (half + 1) * LANES, :] = jnp.concatenate(
                 pieces, 0
             ).astype(jnp.bfloat16)
+    for k in range(1, ntm):
+        stat_copy(k, lax.rem(tm + ntm - k, ntm)).wait_recv()
+    means = [stats[i, 0:1, :] for i in range(ntm)]
+    mean = sum(means[1:], means[0]) * (1.0 / ntm)
+    spread = sum(stats[i, 1:2, :] for i in range(ntm))
+    for i in range(ntm):
+        spread = spread + count * ((means[i] - mean) * (means[i] - mean))
+    var = spread * (1.0 / (count * ntm))
+    scale = lax.rsqrt(var + eps_norm) * mask_ref[...].astype(jnp.float32)
+
+    def carry_copy(rb):
+        return pltpu.make_async_remote_copy(
+            src_ref=carry_out.at[rb],
+            dst_ref=carry_in.at[rb],
+            send_sem=carry_send.at[rb],
+            recv_sem=carry_recv.at[rb],
+            device_id={"tm": lax.rem(tm + 1, ntm)},
+            device_id_type=MESH,
+        )
+
+    def level1(pair, rb):
+        lo = pl.multiple_of(rb * rb_rows, rb_rows)
+        total = None
+        for par in range(2):
+            x = inten[2 * pair + par, pl.ds(lo, rb_rows), :].astype(jnp.float32)
+            normed = ((x - mean) * scale).astype(jnp.bfloat16)
+            term = lax.dot_general(
+                normed, sel1[par], (((1,), (1,)), ((), ())), preferred_element_type=jnp.float32
+            )
+            total = term if total is None else total + term
+        return lo, total
+
+    inv1 = 1.0 / math.sqrt(SUBW)
+    to_row = lax.broadcasted_iota(jnp.int32, (HALF, HALF), 0)
+    from_row = lax.broadcasted_iota(jnp.int32, (HALF, HALF), 1)
+    flip = jnp.where(lax.rem(to_row + from_row, HALF) == 0, 1.0, 0.0).astype(jnp.bfloat16)
+
+    def put_send(pair, lo, total):
+        ready = (total * inv1).astype(jnp.bfloat16)
+        send_buf[pair, pl.ds(lo, HALF), :] = ready[:HALF]
+        send_buf[pair, pl.ds(lo + HALF, HALF), :] = jnp.dot(
+            flip, ready[HALF:], preferred_element_type=jnp.float32
+        ).astype(jnp.bfloat16)
+
+    def turn_copy(pair, k, sender):
+        peer = lax.rem(me + k, ndev)
+        return pltpu.make_async_remote_copy(
+            src_ref=send_buf.at[
+                pair, pl.ds(pl.multiple_of(peer * local_beams, local_beams), local_beams), :
+            ],
+            dst_ref=recv_buf.at[pair, :, pl.ds(pl.multiple_of(sender * LANES, LANES), LANES)],
+            send_sem=turn_send.at[pair, k],
+            recv_sem=turn_recv.at[pair, k],
+            device_id=peer_id(peer),
+            device_id_type=MESH,
+        )
+
+    def own_copy(pair):
+        return pltpu.make_async_copy(
+            send_buf.at[
+                pair, pl.ds(pl.multiple_of(me * local_beams, local_beams), local_beams), :
+            ],
+            recv_buf.at[pair, :, pl.ds(pl.multiple_of(me * LANES, LANES), LANES)],
+            own_sem.at[pair],
+        )
+
+    peers_rb = max(1, ndev // nrb)
+    first_rb = me // peers_rb
+
+    def start_turn(pair, rb):
+        def one(i, carry):
+            k = lax.rem(rb * peers_rb + i + ndev - me, ndev)
+
+            @pl.when(k > 0)
+            def _():
+                turn_copy(pair, k, me).start()
+
+            @pl.when(k == 0)
+            def _():
+                own_copy(pair).start()
+
+            return carry
+
+        lax.fori_loop(0, peers_rb, one, 0)
+
+    last = pairs - 1
+    for pair in range(last, -1, -1):
+
+        def block(i, carry, pair=pair):
+            rb = lax.rem(first_rb + i, nrb)
+            lo, total = level1(pair, rb)
+            if pair == last:
+                carry_out[rb] = total[:, LANES:]
+
+                @pl.when(tm < ntm - 1)
+                def _():
+                    carry_copy(rb).start()
+
+            else:
+                put_send(pair + 1, lo, part_acc[pair + 1, pl.ds(lo, rb_rows), :] + total[:, LANES:])
+                start_turn(pair + 1, rb)
+            part_acc[pair, pl.ds(lo, rb_rows), :] = total[:, :LANES]
+            return carry
+
+        lax.fori_loop(0, nrb, block, 0)
+
     nsubs_all = subs * ndev
     code = (pick_ref[...] + NJ * outer_ref[...]).astype(jnp.float32).astype(jnp.bfloat16)
 
@@ -167,214 +412,20 @@
         return carry
 
     lax.fori_loop(0, ndev, make_sel2, 0)
-    pilot[...] = jnp.zeros_like(pilot)
-    acc1[...] = jnp.zeros_like(acc1)
-    acc2[...] = jnp.zeros_like(acc2)
-
-    @pl.when(tm == 0)
-    def _():
-        carry_in[...] = jnp.zeros_like(carry_in)
-        carry2_in[...] = jnp.zeros_like(carry2_in)
-
-    def transform(step, field):
-        volt_copy(step).wait()
-        for e in range(EW):
-            block = vbuf[step, :, e * NS : (e + 1) * NS, :].reshape(2 * NS, ct)
-            field[e] = jnp.dot(table_ref[...], block, preferred_element_type=jnp.float32)
-
-    CH = 16
-
-    def fold8(x):
-        return x[:8] + x[8:]
-
-    def detect(step, field):
-        t, tile = step // ctiles, lax.rem(step, ctiles)
-        shift = jnp.broadcast_to(pilot[tile], (CH, ct))
-        s1 = jnp.zeros((8, ct), jnp.float32)
-        s2 = jnp.zeros((8, ct), jnp.float32)
-        col = pl.ds(pl.multiple_of(tile * ct, ct), ct)
-        for chunk in range(NS // CH):
-            lo = chunk * CH
-            re = [field[e, lo : lo + CH, :] for e in range(EW)]
-            im = [field[e, NS + lo : NS + lo + CH, :] for e in range(EW)]
-            ra, rb, rc, rd = re[0] + re[2], re[0] - re[2], re[1] + re[3], re[1] - re[3]
-            ia, ib, ic, id_ = im[0] + im[2], im[0] - im[2], im[1] + im[3], im[1] - im[3]
-            beam = [
-                (ra + rc, ia + ic),
-                (rb + id_, ib - rd),
-                (ra - rc, ia - ic),
-                (rb - id_, ib + rd),
-            ]
-            for q in range(EW):
-                x = beam[q][0] * beam[q][0] + beam[q][1] * beam[q][1]
-                x = x.astype(jnp.bfloat16)
-                inten[t, q * NS + lo : q * NS + lo + CH, col] = x
-                dev = x.astype(jnp.float32) - shift
-                s1 = s1 + fold8(dev)
-                s2 = s2 + fold8(dev * dev)
-
-        @pl.when(t > 0)
-        def _():
-            acc1[tile] += s1
-            acc2[tile] += s2
-
-        @pl.when(t == 0)
-        def _():
-            mean = jnp.sum(s1, axis=0, keepdims=True) * (1.0 / BEAMS)
-            pilot[tile] = mean
-            wide = jnp.broadcast_to(mean, (CH, ct))
-
-            def again(chunk, sums):
-                r1, r2 = sums
-                lo = pl.multiple_of(chunk * 4 * CH, 4 * CH)
-                for i in range(4):
-                    x = inten[0, pl.ds(lo + i * CH, CH), col].astype(jnp.float32)
-                    dev = x - wide
-                    r1 = r1 + fold8(dev)
-                    r2 = r2 + fold8(dev * dev)
-                return r1, r2
-
-            zero = jnp.zeros((8, ct), jnp.float32)
-            r1, r2 = lax.fori_loop(0, BEAMS // (4 * CH), again, (zero, zero))
-            acc1[tile] = r1
-            acc2[tile] = r2
-
-    transform(0, field0)
-
-    def two_steps(i, carry):
-        transform(2 * i + 1, field1)
-        detect(2 * i, field0)
-
-        @pl.when(2 * i + 2 < steps)
-        def _():
-            transform(2 * i + 2, field0)
-
-        detect(2 * i + 1, field1)
-        return carry
-
-    lax.fori_loop(0, steps // 2, two_steps, 0)
-
-    count = float(rows * BEAMS)
-    for tile in range(ctiles):
-        s1 = jnp.sum(acc1[tile], axis=0, keepdims=True)
-        s2 = jnp.sum(acc2[tile], axis=0, keepdims=True)
-        cols = slice(tile * ct, (tile + 1) * ct)
-        stats[tm, 0:1, cols] = pilot[tile] + s1 * (1.0 / count)
-        stats[tm, 1:2, cols] = s2 - s1 * s1 * (1.0 / count)
-
-    pl.semaphore_wait(barrier, ntm - 1 + ndev - 1)
-
-    def stat_copy(k, sender):
-        return pltpu.make_async_remote_copy(
-            src_ref=stats.at[tm],
-            dst_ref=stats.at[sender],
-            send_sem=stat_send.at[k],
-            recv_sem=stat_recv.at[k],
-            device_id={"tm": lax.rem(tm + k, ntm)},
-            device_id_type=MESH,
-        )
-
-    for k in range(1, ntm):
-        stat_copy(k, tm).start()
-    for k in range(1, ntm):
-        stat_copy(k, lax.rem(tm + ntm - k, ntm)).wait_recv()
-    means = [stats[i, 0:1, :] for i in range(ntm)]
-    mean = sum(means[1:], means[0]) * (1.0 / ntm)
-    spread = sum(stats[i, 1:2, :] for i in range(ntm))
-    for i in range(ntm):
-        spread = spread + count * ((means[i] - mean) * (means[i] - mean))
-    var = spread * (1.0 / (count * ntm))
-    scale = lax.rsqrt(var + eps_norm) * mask_ref[...].astype(jnp.float32)
-
-    def carry_copy(rb):
-        return pltpu.make_async_remote_copy(
-            src_ref=carry_out.at[rb],
-            dst_ref=carry_in.at[rb],
-            send_sem=carry_send.at[rb],
-            recv_sem=carry_recv.at[rb],
-            device_id={"tm": lax.rem(tm + 1, ntm)},
-            device_id_type=MESH,
-        )
-
-    def level1(pair, rb):
-        lo = pl.multiple_of(rb * rb_rows, rb_rows)
-        total = None
-        for par in range(2):
-            x = inten[2 * pair + par, pl.ds(lo, rb_rows), :].astype(jnp.float32)
-            normed = ((x - mean) * scale).astype(jnp.bfloat16)
-            term = lax.dot_general(
-                normed, sel1[par], (((1,), (1,)), ((), ())), preferred_element_type=jnp.float32
-            )
-            total = term if total is None else total + term
-        return lo, total
-
-    inv1 = 1.0 / math.sqrt(SUBW)
-
-    def put_send(pair, lo, total):
-        send_buf[pair, pl.ds(lo, rb_rows), :] = (total * inv1).astype(jnp.bfloat16)
-
-    def turn_copy(pair, k, sender):
-        peer = lax.rem(me + k, ndev)
-        return pltpu.make_async_remote_copy(
-            src_ref=send_buf.at[
-                pair, pl.ds(pl.multiple_of(peer * local_beams, local_beams), local_beams), :
-            ],
-            dst_ref=recv_buf.at[pair, :, pl.ds(pl.multiple_of(sender * LANES, LANES), LANES)],
-            send_sem=turn_send.at[pair, k],
-            recv_sem=turn_recv.at[pair, k],
-            device_id=peer_id(peer),
-            device_id_type=MESH,
-        )
-
-    def own_copy(pair):
-        return pltpu.make_async_copy(
-            send_buf.at[
-                pair, pl.ds(pl.multiple_of(me * local_beams, local_beams), local_beams), :
-            ],
-            recv_buf.at[pair, :, pl.ds(pl.multiple_of(me * LANES, LANES), LANES)],
-            own_sem.at[pair],
-        )
-
-    def start_turn(pair):
-        def one(k, carry):
-            turn_copy(pair, k, me).start()
-            return carry
-
-        lax.fori_loop(1, ndev, one, 0)
-        own_copy(pair).start()
-
-    last = pairs - 1
-    for pair in range(last, -1, -1):
-
-        def block(rb, carry, pair=pair):
-            lo, total = level1(pair, rb)
-            if pair == last:
-                carry_out[rb] = total[:, LANES:]
-
-                @pl.when(tm < ntm - 1)
-                def _():
-                    carry_copy(rb).start()
-
-            else:
-                put_send(pair + 1, lo, part_acc[pair + 1, pl.ds(lo, rb_rows), :] + total[:, LANES:])
-            part_acc[pair, pl.ds(lo, rb_rows), :] = total[:, :LANES]
-            return carry
-
-        lax.fori_loop(0, nrb, block, 0)
-        if pair < last:
-            start_turn(pair + 1)
-
-    def finish(rb, carry):
+
+    def finish(i, carry):
+        rb = lax.rem(first_rb + i, nrb)
+
         @pl.when(tm > 0)
         def _():
             carry_copy(rb).wait_recv()
 
         lo = pl.multiple_of(rb * rb_rows, rb_rows)
         put_send(0, lo, part_acc[0, pl.ds(lo, rb_rows), :] + carry_in[rb])
+        start_turn(0, rb)
         return carry
 
     lax.fori_loop(0, nrb, finish, 0)
-    start_turn(0)
 
     carry2_copy = pltpu.make_async_remote_copy(
         src_ref=carry2_out,

time: 50.6 us -> 39.1 us (0.77)
  Pallas kernels: 48.4 us -> 37.2 us
    pallas_call x1, Pallas kernels: 48.4 us -> 37.2 us  [body(): pl.pallas_call(functools.partial(kernel, cfg), out_shape=jax.ShapeDtypeSt...]
where the time goes in v2:
time: 39.1 us; the launch traced here: 38.9 us
  Pallas kernels  37.2 us (95%)
  local copies, waits for them, and re-layouts  1.67 us (4%)
    pallas_call x1, Pallas kernels, body(): pl.pallas_call(functools.partial(kernel, cfg), out_shape=jax.ShapeDtypeSt...  37.2 us
    unnamed x1, local copies, waits for them, and re-layouts  1.67 us

profile of v2, /device:TPU:11, one launch (start us, length us, event | category | flops | bytes accessed | tf_op | source)
XLA Modules:
  0.0 38.9 jit_solution(3709725871685447352)
XLA Ops:
  0.0 37.2 %shard_map.64 = f32[4,128,128]{2,1,0:T(8,128)} custom-call(bf16[2,4,1024,1024]{3,2,1,0:T(8,128)(2,1)} %volt_hbm.1, bf16[256,256]{1,0:T(8,128)(2,1)} %constant.2.clone.table_ref, s32[1,1024]{1,0:T(1,128)} %bitcast.3, s32[8,8192]{1,0:T(8,128)} %bitcast.2, s32[64,128]{1,0:T(8,128)} %pick_ref.1, s32[64,128]{1,0:T(8,128)} %outer_ref.1), custom_call_target="tpu_custom_call" | custom-call | tf_op jit(solution)/shard_map/pallas_call | solution.py:507
  37.2 1.7 %copy.8 = f32[4,128,128]{2,1,0:T(8,128)} copy(f32[4,128,128]{2,1,0:T(8,128)} %shard_map.64) | data formatting | bytes 524288

commit v3 on v2

--- a/solution.py
+++ b/solution.py
@@ -141,10 +141,7 @@
                     table_ref[...], block, preferred_element_type=jnp.float32
                 )
 
-    CH, HALF = 16, NS // 2
-
-    def fold8(x):
-        return x[:8] + x[8:]
+    CH, HALF = 8, NS // 2
 
     def detect(step, field):
         t, tile = step // ctiles, lax.rem(step, ctiles)
@@ -194,8 +191,8 @@
                         at = q * NS + mirror * HALF + lo
                         inten[t, at : at + CH, here] = x
                         dev = x.astype(jnp.float32) - shift
-                        s1 = s1 + fold8(dev)
-                        s2 = s2 + fold8(dev * dev)
+                        s1 = s1 + dev
+                        s2 = s2 + dev * dev
             sums1.append(s1)
             sums2.append(s2)
         s1, s2 = jnp.concatenate(sums1, 1), jnp.concatenate(sums2, 1)
@@ -209,20 +206,21 @@
         def _():
             mean = jnp.sum(s1, axis=0, keepdims=True) * (1.0 / BEAMS)
             pilot[tile] = mean
-            wide = jnp.broadcast_to(mean, (CH, ct))
+            wide = jnp.broadcast_to(mean, (16, ct))
 
             def again(chunk, sums):
                 r1, r2 = sums
-                lo = pl.multiple_of(chunk * 4 * CH, 4 * CH)
+                lo = pl.multiple_of(chunk * 64, 64)
                 for i in range(4):
-                    x = inten[0, pl.ds(lo + i * CH, CH), col].astype(jnp.float32)
+                    x = inten[0, pl.ds(lo + i * 16, 16), col].astype(jnp.float32)
                     dev = x - wide
-                    r1 = r1 + fold8(dev)
-                    r2 = r2 + fold8(dev * dev)
+                    sq = dev * dev
+                    r1 = r1 + (dev[:8] + dev[8:])
+                    r2 = r2 + (sq[:8] + sq[8:])
                 return r1, r2
 
             zero = jnp.zeros((8, ct), jnp.float32)
-            r1, r2 = lax.fori_loop(0, BEAMS // (4 * CH), again, (zero, zero))
+            r1, r2 = lax.fori_loop(0, BEAMS // 64, again, (zero, zero))
             acc1[tile] = r1
             acc2[tile] = r2
 
@@ -366,25 +364,27 @@
         lax.fori_loop(0, peers_rb, one, 0)
 
     last = pairs - 1
-    for pair in range(last, -1, -1):
-
-        def block(i, carry, pair=pair):
-            rb = lax.rem(first_rb + i, nrb)
+    def block(i, carry):
+        rb = lax.rem(first_rb + i + 1, nrb)
+        held = None
+        for pair in range(last, -1, -1):
             lo, total = level1(pair, rb)
             if pair == last:
                 carry_out[rb] = total[:, LANES:]
-
-                @pl.when(tm < ntm - 1)
-                def _():
-                    carry_copy(rb).start()
-
             else:
-                put_send(pair + 1, lo, part_acc[pair + 1, pl.ds(lo, rb_rows), :] + total[:, LANES:])
-                start_turn(pair + 1, rb)
-            part_acc[pair, pl.ds(lo, rb_rows), :] = total[:, :LANES]
-            return carry
-
-        lax.fori_loop(0, nrb, block, 0)
+                put_send(pair + 1, lo, held + total[:, LANES:])
+            held = total[:, :LANES]
+        part_acc[rb] = held
+
+        @pl.when(tm < ntm - 1)
+        def _():
+            carry_copy(rb).start()
+
+        for pair in range(last, 0, -1):
+            start_turn(pair, rb)
+        return carry
+
+    lax.fori_loop(0, nrb, block, 0)
 
     nsubs_all = subs * ndev
     code = (pick_ref[...] + NJ * outer_ref[...]).astype(jnp.float32).astype(jnp.bfloat16)
@@ -414,14 +414,14 @@
     lax.fori_loop(0, ndev, make_sel2, 0)
 
     def finish(i, carry):
-        rb = lax.rem(first_rb + i, nrb)
+        rb = lax.rem(first_rb + i + 1, nrb)
 
         @pl.when(tm > 0)
         def _():
             carry_copy(rb).wait_recv()
 
         lo = pl.multiple_of(rb * rb_rows, rb_rows)
-        put_send(0, lo, part_acc[0, pl.ds(lo, rb_rows), :] + carry_in[rb])
+        put_send(0, lo, part_acc[rb] + carry_in[rb])
         start_turn(0, rb)
         return carry
 
@@ -521,7 +521,7 @@
             pltpu.VMEM((ctiles, 8, ct), f32),
             pltpu.VMEM((ctiles, 8, ct), f32),
             pltpu.VMEM((ntm, 2, chans), f32),
-            pltpu.VMEM((pairs, BEAMS, LANES), f32),
+            pltpu.VMEM((nrb, rb, LANES), f32),
             pltpu.VMEM((nrb, rb, LANES), f32),
             pltpu.VMEM((nrb, rb, LANES), f32),
             pltpu.VMEM((pairs, BEAMS, LANES), bf16),

time: 39.1 us -> 35.8 us (0.916)
  Pallas kernels: 37.2 us -> 33.9 us
    pallas_call x1, Pallas kernels: 37.2 us -> 33.9 us  [body(): pl.pallas_call(functools.partial(kernel, cfg), out_shape=jax.ShapeDtypeSt...]
where the time goes in v3:
time: 35.8 us; the launch traced here: 35.6 us
  Pallas kernels  33.9 us (95%)
  local copies, waits for them, and re-layouts  1.67 us (5%)
    pallas_call x1, Pallas kernels, body(): pl.pallas_call(functools.partial(kernel, cfg), out_shape=jax.ShapeDtypeSt...  33.9 us
    unnamed x1, local copies, waits for them, and re-layouts  1.67 us

profile of v3, /device:TPU:11, one launch (start us, length us, event | category | flops | bytes accessed | tf_op | source)
XLA Modules:
  0.0 35.6 jit_solution(12832568987240930207)
XLA Ops:
  0.0 33.9 %shard_map.64 = f32[4,128,128]{2,1,0:T(8,128)} custom-call(bf16[2,4,1024,1024]{3,2,1,0:T(8,128)(2,1)} %volt_hbm.1, bf16[256,256]{1,0:T(8,128)(2,1)} %constant.2.clone.table_ref, s32[1,1024]{1,0:T(1,128)} %bitcast.3, s32[8,8192]{1,0:T(8,128)} %bitcast.2, s32[64,128]{1,0:T(8,128)} %pick_ref.1, s32[64,128]{1,0:T(8,128)} %outer_ref.1), custom_call_target="tpu_custom_call" | custom-call | tf_op jit(solution)/shard_map/pallas_call | solution.py:507
  33.9 1.7 %copy.8 = f32[4,128,128]{2,1,0:T(8,128)} copy(f32[4,128,128]{2,1,0:T(8,128)} %shard_map.64) | data formatting | bytes 524288

commit v4 on v3

--- a/solution.py
+++ b/solution.py
@@ -35,12 +35,16 @@
 def kernel(
     cfg,
     volt_hbm,
+    table_hbm,
+    mask_hbm,
+    delay_hbm,
+    pick_hbm,
+    outer_hbm,
+    out_ref,
     table_ref,
     mask_ref,
-    delay_hbm,
     pick_ref,
     outer_ref,
-    out_ref,
     vbuf,
     inten,
     field0,
@@ -59,6 +63,7 @@
     recv_buf,
     carry2_out,
     carry2_in,
+    small_sem,
     vsem,
     dsem,
     stat_send,
@@ -96,6 +101,12 @@
             vsem.at[step],
         )
 
+    table_copy = pltpu.make_async_copy(table_hbm, table_ref, small_sem.at[0])
+    mask_copy = pltpu.make_async_copy(mask_hbm, mask_ref, small_sem.at[1])
+    pick_copy = pltpu.make_async_copy(pick_hbm, pick_ref, small_sem.at[2])
+    outer_copy = pltpu.make_async_copy(outer_hbm, outer_ref, small_sem.at[3])
+    table_copy.start()
+
     def start_volt(step, carry):
         volt_copy(step).start()
         return carry
@@ -105,6 +116,9 @@
         delay_hbm.at[:, pl.ds(pl.multiple_of(me * chans, chans), chans)], delay_v, dsem
     )
     delay_copy.start()
+    mask_copy.start()
+    pick_copy.start()
+    outer_copy.start()
 
     barrier = pltpu.get_barrier_semaphore()
 
@@ -224,6 +238,7 @@
             acc1[tile] = r1
             acc2[tile] = r2
 
+    table_copy.wait()
     transform(0, field0)
 
     def two_steps(i, carry):
@@ -262,6 +277,9 @@
     for k in range(1, ntm):
         stat_copy(k, tm).start()
     delay_copy.wait()
+    mask_copy.wait()
+    pick_copy.wait()
+    outer_copy.wait()
     delays = delay_v[...].astype(jnp.float32)
     chan_sub = lax.broadcasted_iota(jnp.int32, (NJ, chans), 1) // SUBW
     for par_in in range(2):
@@ -507,9 +525,13 @@
     return pl.pallas_call(
         functools.partial(kernel, cfg),
         out_shape=jax.ShapeDtypeStruct((rows, lb, ndm), f32),
-        in_specs=[hbm, vm, vm, hbm, vm, vm],
+        in_specs=[hbm] * 6,
         out_specs=vm,
         scratch_shapes=[
+            pltpu.VMEM((NS, NS), bf16),
+            pltpu.VMEM((1, chans), jnp.int32),
+            pltpu.VMEM(pick.shape, jnp.int32),
+            pltpu.VMEM(outer_delay.shape, jnp.int32),
             pltpu.VMEM((steps, 2, EW * NS, ct), bf16),
             pltpu.VMEM((rows, BEAMS, chans), bf16),
             pltpu.VMEM((EW, 2 * NS, ct), f32),
@@ -528,6 +550,7 @@
             pltpu.VMEM((pairs, lb, ndev * LANES), bf16),
             pltpu.VMEM((lb, 2 * ndm), f32),
             pltpu.VMEM((lb, 2 * ndm), f32),
+            dma((4,)),
             dma((steps,)),
             dma,
             dma((ntm,)),

time: 35.8 us -> 35 us (0.978)
  Pallas kernels: 33.9 us -> 33.1 us
    pallas_call x1, Pallas kernels: 33.9 us -> 33.1 us  [body(): pl.pallas_call(functools.partial(kernel, cfg), out_shape=jax.ShapeDtypeSt...]
where the time goes in v4:
time: 35 us; the launch traced here: 34.8 us
  Pallas kernels  33.1 us (95%)
  local copies, waits for them, and re-layouts  1.67 us (5%)
    pallas_call x1, Pallas kernels, body(): pl.pallas_call(functools.partial(kernel, cfg), out_shape=jax.ShapeDtypeSt...  33.1 us
    unnamed x1, local copies, waits for them, and re-layouts  1.67 us

profile of v4, /device:TPU:11, one launch (start us, length us, event | category | flops | bytes accessed | tf_op | source)
XLA Modules:
  0.0 34.8 jit_solution(10972727315879007601)
XLA Ops:
  0.0 33.1 %shard_map.64 = f32[4,128,128]{2,1,0:T(8,128)} custom-call(bf16[2,4,1024,1024]{3,2,1,0:T(8,128)(2,1)} %volt_hbm.1, bf16[256,256]{1,0:T(8,128)(2,1)} %constant.2.clone.table_hbm, s32[1,1024]{1,0:T(1,128)} %bitcast.3, s32[8,8192]{1,0:T(8,128)} %bitcast.2, s32[64,128]{1,0:T(8,128)} %pick_hbm.1, s32[64,128]{1,0:T(8,128)} %outer_hbm.1), custom_call_target="tpu_custom_call" | custom-call | tf_op jit(solution)/shard_map/pallas_call | solution.py:525
  33.1 1.7 %copy.8 = f32[4,128,128]{2,1,0:T(8,128)} copy(f32[4,128,128]{2,1,0:T(8,128)} %shard_map.64) | data formatting | bytes 524288
